TPU v7x, 256 devices: a whole 4x4x8 slice. The times are simulated.
256 devices in a mesh: tm: 32 (over x, z_hi, core), head: 8 (over z_lo, y).
Axes of the slice: x: 4, y: 4, z: 8 (z_hi: 4, z_lo: 2; z = z_hi * 2 + z_lo), core: 2. Of those that a mesh axis runs over, the one named last changes fastest.
Arguments:
- query_states: bfloat16 [49152, 1024], P('tm', 'head'), may hold values from -30 to 30
- key_states: bfloat16 [49152, 1024], P('tm', 'head'), may hold values from -30 to 30
- value_states: bfloat16 [49152, 1024], P('tm', 'head'), may hold values from -6 to 6
- win_start: int32 [64], P('tm'), may hold values from 0 to 62, as said below
- group_end: int32 [64], P('tm'), may hold values from 0 to 63, as said below
- out_weight: bfloat16 [1024, 1536], replicated, may hold values from -0.1875 to 0.1875
Outputs:
- projected: bfloat16 [49152, 1536], P(('tm', 'head'))
Inputs may be any that keep to these rules, and one draw needn't show every extreme that they name: For every frame f, win_start[f] = max(f - lag, 0) with a lag of 1 to 3; frame 64 - 2 has a lag of 3 in every draw, and the last frame has a lag of 1. `group_end`: frames 2p and 2p + 1 form one group (both end at 2p + 1) or two groups of one frame (each ends at itself); both kinds occur in every draw.
All inputs are finite; a program needn't handle non-finite values.
Results may differ from a plain program's by a relative error of at most 0.0051.
Values may be sent and summed in bfloat16 or wider, within the bound.
A program may use at most 64 MiB of HBM per device.

v0:
```python
import jax
import jax.numpy as jnp
from jax import lax
from jax.sharding import PartitionSpec as P

HD = 128
FT = 768


def spread(block, axis, owner):
    block = jnp.where(lax.axis_index(axis) == owner, block, jnp.zeros_like(block))
    return lax.psum(block, axis)


def from_behind(array, axis, by):
    length = lax.axis_size(axis)
    pairs = [(i, i + by) for i in range(length) if 0 <= i + by < length]
    return lax.ppermute(array, axis, pairs)


def attend(query_rows, key_rows, value_rows, visible):
    heads_here = query_rows.shape[1] // HD
    query_heads = query_rows.reshape(query_rows.shape[0], heads_here, HD)
    key_heads = key_rows.reshape(key_rows.shape[0], heads_here, HD)
    value_heads = value_rows.reshape(value_rows.shape[0], heads_here, HD)
    scores = jnp.einsum(
        "qhd,khd->hqk", query_heads, key_heads, preferred_element_type=jnp.float32
    ) * HD ** (-0.5)
    scores = jnp.where(visible[None, None, :], scores, -1e30)
    peak = jnp.max(scores, axis=-1, keepdims=True)
    weights = jnp.where(visible[None, None, :], jnp.exp(scores - peak), 0.0)
    total = jnp.sum(weights, axis=-1)
    rounded = weights.astype(jnp.bfloat16)
    mixed = jnp.einsum("hqk,khd->qhd", rounded, value_heads, preferred_element_type=jnp.float32)
    mixed = mixed / jnp.transpose(total)[:, :, None]
    return mixed.astype(jnp.bfloat16).reshape(query_rows.shape[0], query_rows.shape[1])


def local(query_states, key_states, value_states, win_start, group_end, out_weight):
    local_frames = win_start.shape[0]
    stacked = jnp.stack([key_states, value_states])
    sink_frame = stacked[:, :FT]
    sink_states = spread(sink_frame, "tm", 0)
    near_count = min(3, local_frames)
    far_count = 3 - near_count
    near_frames = from_behind(stacked, "tm", 1)
    pieces = []
    far_frames = from_behind(stacked[:, (local_frames - far_count) * FT :], "tm", 2)
    pieces.append(far_frames)
    extended = jnp.concatenate(pieces + [near_frames, stacked], axis=1)
    first_id = lax.axis_index("tm") * local_frames - 3
    outputs = []
    for slot in range(local_frames):
        span_frames = 5 if slot % 2 == 0 else 4
        window = extended[:, slot * FT : (slot + span_frames) * FT]
        key_rows = jnp.concatenate([sink_states[0], window[0]], axis=0)
        value_rows = jnp.concatenate([sink_states[1], window[1]], axis=0)
        frame_ids = first_id + slot + jnp.arange(span_frames * FT, dtype=jnp.int32) // FT
        window_seen = (
            (frame_ids >= 1) & (frame_ids >= win_start[slot]) & (frame_ids <= group_end[slot])
        )
        visible = jnp.concatenate([jnp.ones((FT,), dtype=bool), window_seen])
        query_rows = query_states[slot * FT : (slot + 1) * FT]
        outputs.append(attend(query_rows, key_rows, value_rows, visible))
    attended = jnp.concatenate(outputs, axis=0)
    token_rows = lax.all_to_all(attended, "head", split_axis=0, concat_axis=1, tiled=True)
    return jnp.dot(token_rows, out_weight, preferred_element_type=jnp.float32).astype(jnp.bfloat16)


def solution(mesh):
    in_specs = (P("tm", "head"), P("tm", "head"), P("tm", "head"), P("tm"), P("tm"), P())
    out_specs = P(("tm", "head"), None)
    return jax.shard_map(local, mesh=mesh, in_specs=in_specs, out_specs=out_specs, check_vma=False)
```

profile of v0, /device:TPU:8, one launch (start us, length us, event | category | flops | bytes accessed | tf_op | source)
XLA Modules:
  0.0 344.9 jit_solution(8197452554077602024)
XLA Ops:
  6.5 0.0 copy-start
  6.5 0.0 copy-start.1
  6.5 0.0 all-reduce.4.cloned.1.call-start
  6.5 2.2 pad_maximum_fusion
  8.8 2.6 collective-permute-start.1
  11.4 2.2 fusion.58
  13.6 0.0 all-reduce.4.cloned.1.call-update
  13.6 5.2 %collective-permute-start = (bf16[2,768,128]{2,1,0:T(8,128)(2,1)}, bf16[2,768,128]{2,1,0:T(8,128)(2,1)}, u32[]{:S(2)}, u32[]{:S(2)}) collective-permute-start(bf16[2,768,128]{2,1,0:T(8,128)(2,1)} %get-tuple-element.9), channel_id=1, source_target_pairs={{0,16},{8,24},{16,32},{24,40},{32,48},{40,56},{48,64},{56,72},{64,... | collective-permute-start | bytes 1179656 | tf_op jit(solution)/shard_map/ppermute | solution.py:18
  18.8 1.3 fusion.81
  20.2 1.3 fusion.82
  21.4 1.1 compare_and_fusion.1
  22.6 1.2 compare_and_fusion
  23.8 275.4 %all-reduce.4.cloned.1.call-done = bf16[2,768,128]{2,1,0:T(8,128)(2,1)} async-done(((bf16[2,768,128]{2,1,0:T(8,128)(2,1)}), bf16[2,768,128]{2,1,0:T(8,128)(2,1)}) %all-reduce.4.cloned.1.call-update) | async-done | bytes 393232 | tf_op jit(solution)/shard_map/psum | solution.py:12
  299.2 0.0 copy-start.2
  299.2 1.1 slice_bitcast_fusion.5
  300.3 0.0 collective-permute-done.1
  300.3 1.5 maximum_maximum_fusion.1
  301.8 0.0 copy-start.3
  301.8 0.1 slice_bitcast_fusion.3
  301.9 0.0 collective-permute-done
  301.9 0.0 copy-done.1
  301.9 0.0 copy-done.2
  301.9 1.4 maximum_maximum_fusion
  303.3 0.1 slice_bitcast_fusion.1
  303.4 0.0 copy-done.3
  303.4 1.9 fusion.1
  305.4 3.9 %fusion.4 = f32[768]{0:T(1024)S(1)} fusion(f32[3840,768]{1,0:T(8,128)S(1)} %get-tuple-element.18, f32[768]{0:T(1024)S(1)} %get-tuple-element.17, pred[3840]{0:T(1024)(128)(4,1)S(1)} %concatenate.33), kind=kLoop, calls=%fused_computation.8 | loop fusion | flops 14744832 | bytes 11806464 | tf_op jit(solution)/shard_map/reduce_sum | solution.py:32
  309.3 2.3 fusion
  311.6 4.5 %fusion.2 = f32[768]{0:T(1024)S(1)} fusion(f32[4608,768]{1,0:T(8,128)S(1)} %get-tuple-element.20, f32[768]{0:T(1024)S(1)} %get-tuple-element.19, pred[4608]{0:T(1024)(128)(4,1)S(1)} %concatenate.29), kind=kLoop, calls=%fused_computation.6 | loop fusion | flops 17693952 | bytes 14166528 | tf_op jit(solution)/shard_map/reduce_sum | solution.py:32
  316.1 3.2 fusion.46
  319.4 3.8 %fusion.35 = bf16[768,128]{0,1:T(8,128)(2,1)S(1)} fusion(f32[4608,768]{1,0:T(8,128)S(1)} %get-tuple-element.20, f32[768]{0:T(1024)S(1)} %get-tuple-element.19, pred[4608]{0:T(1024)(128)(4,1)S(1)} %concatenate.29, bf16[3840,128]{1,0:T(8,128)(2,1)S(1)} %get-tuple-element.5, bf16[768,128]{1,0:T(8,128)(2,1)S(1)} %get-tuple-element.11, f32[768]{0:T(1024)S(1)} %fusion.2), kind=kOutput, calls=%fused_computation.28 | convolution fusion | flops 926220288 | bytes 15542784 | tf_op jit(solution)/shard_map/hqk,khd->qhd/dot_general | solution.py:34
  323.3 0.9 copy.7
  324.2 12.3 %all_to_all.19 = bf16[8,192,128]{2,1,0:T(8,128)(2,1)S(1)} all-to-all(bf16[8,192,128]{2,1,0:T(8,128)(2,1)} %bitcast.60), channel_id=1, replica_groups=mesh['tm'=32,'head'=8] {'head'}, dimensions={0} | all-to-all | bytes 786432 | tf_op jit(solution)/shard_map/all_to_all | solution.py:66
  336.5 0.0 copy-done
  336.5 1.6 convolution_convert_fusion
  (3 shorter events, 0.0 us)
Async XLA Ops:
  6.5 329.9 %copy-start = (bf16[1024,1536]{1,0:T(8,128)(2,1)S(1)}, bf16[1024,1536]{1,0:T(8,128)(2,1)}, u32[]{:S(2)}) copy-start(bf16[1024,1536]{1,0:T(8,128)(2,1)} %param.11) | copy-start | bytes 9437188
  6.5 295.4 %copy-start.1 = (bf16[1536,128]{1,0:T(8,128)(2,1)S(1)}, bf16[1536,128]{1,0:T(8,128)(2,1)}, u32[]{:S(2)}) copy-start(bf16[1536,128]{1,0:T(8,128)(2,1)} %param.8) | copy-start | bytes 1179652
  6.5 292.6 %all-reduce.4.cloned.1.call-start = ((), (), s32[]{:S(2)}) async-start(), calls=%async_computation.1 | async-start | bytes 786432 | tf_op jit(solution)/shard_map/psum | solution.py:12
  8.8 291.5 %collective-permute-start.1 = (bf16[2,1536,128]{2,1,0:T(8,128)(2,1)}, bf16[2,1536,128]{2,1,0:T(8,128)(2,1)}, u32[]{:S(2)}, u32[]{:S(2)}) collective-permute-start(bf16[2,1536,128]{2,1,0:T(8,128)(2,1)} %pad_maximum_fusion), channel_id=1, source_target_pairs={{0,8},{8,16},{16,24},{24,32},{32,40},{40,48},{48,56},{56,64},{64,7... | collective-permute-start | bytes 2359304 | tf_op jit(solution)/shard_map/ppermute | solution.py:18
  13.6 288.3 %collective-permute-start = (bf16[2,768,128]{2,1,0:T(8,128)(2,1)}, bf16[2,768,128]{2,1,0:T(8,128)(2,1)}, u32[]{:S(2)}, u32[]{:S(2)}) collective-permute-start(bf16[2,768,128]{2,1,0:T(8,128)(2,1)} %get-tuple-element.9), channel_id=1, source_target_pairs={{0,16},{8,24},{16,32},{24,40},{32,48},{40,56},{48,64},{56,72},{64,... | collective-permute-start | bytes 1179656 | tf_op jit(solution)/shard_map/ppermute | solution.py:18
  299.2 2.7 copy-start.2
  301.8 1.7 copy-start.3
Sparse Core Ops, SparseCore 0:
  13.7 285.4 all-reduce.3
where the time goes:
time: 345 us
  waiting for transfers between devices  275 us (80%)
  other arithmetic  18 us (5%)
  between operations  13.5 us (4%)
  matrix products  12.9 us (4%)
  blocking collectives  12.3 us (4%)
  starting transfers between devices  7.88 us (2%)
  local copies, waits for them, and re-layouts  4.87 us (1%)
    psum x1, waiting for transfers between devices, spread(): return lax.psum(block, axis)  275 us
    all_to_all x1, blocking collectives, local(): lax.all_to_all(attended, 'head', split_axis=0, concat_axis=1, tiled=True)  12.3 us
    reduce_sum x2, other arithmetic, attend(): total = jnp.sum(weights, axis=-1)  8.39 us
    ppermute x2, starting transfers between devices, from_behind(): return lax.ppermute(array, axis, pairs)  7.88 us
    dot_general x2, matrix products, attend(): jnp.einsum('hqk,khd->qhd', rounded, value_heads, preferred_element_type=j...  7.06 us
  transfers between devices with their start and end apart: 3, of which 1 were waited for; matrix products, arithmetic and copies ran while one was open for 3% of the time, Pallas kernels for 0%

commit v1 on v0

v1 whole, which is shorter than its diff:
```python
import jax
import jax.numpy as jnp
from jax import lax
from jax.experimental import pallas as pl
from jax.experimental.pallas import tpu as pltpu
from jax.sharding import PartitionSpec as P

HD = 128
FT = 768
BLK = 192
C = HD**-0.5 * 1.4426950408889634
HIDE = -1.0e6
LOW = -3.0e6
MESH = pl.DeviceIdType.MESH

Q0 = (0, 1, 0, 1, 2, 2, 3, 0, 1, 0, 1)
K0 = (0, 0, 1, 1, 1, 2, 2, 4, 4, 5, 5)
Q1 = (0, 1, 0, 1, 0, 1, 0, 1, 1, 0, 0)
K1 = (0, 0, 1, 1, 2, 2, 3, 3, 5, 5, 4)

PK0, PV0, PK1, PV1, TK, TV, RQ0, RQ1, RB, RO, RT, SK, SV, RH = (
    0, 1, 2, 3, 4, 5, 6, 7, 8, 9, 11, 13, 17, 21)
S1S, S2S, S3S, SH = 13, 19, 25, 39


def kernel(q_hbm, k_hbm, v_hbm, ws, ge, out_ref, qb, kb, vb, acc, mm, s0, s1, x0, x1,
           bt, bs, att, ro, rs, reto, rets, gath, lsem, ssem, rsem):
    tm = lax.axis_index("tm")
    hd = lax.axis_index("head")
    core = lax.rem(tm, 2)
    c = lax.div(tm, 2)
    x = lax.div(c, 4)
    zh = lax.rem(c, 4)
    other = tm + 1 - 2 * core
    has_prev = c > 0
    has_next = c < 15
    first = (c == 0).astype(jnp.int32)
    last = (c == 15).astype(jnp.int32)
    is0 = core == 0
    is1 = core == 1

    def both(*conds):
        r = conds[0]
        for d in conds[1:]:
            r = jnp.logical_and(r, d)
        return r

    def rc(src, dst, si, ri, t, h):
        return pltpu.make_async_remote_copy(
            src_ref=src, dst_ref=dst, send_sem=ssem.at[si], recv_sem=rsem.at[ri],
            device_id=(t, h), device_id_type=MESH)

    def got(dst, ri):
        rc(dst, dst, 0, ri, other, hd).wait_recv()

    def sent(src, si):
        rc(src, src, si, 0, other, hd).wait_send()

    def kf(n):
        return kb.at[pl.ds(n * FT, FT)]

    def vf(n):
        return vb.at[pl.ds(n * FT, FT), pl.ds(0, HD)]

    def kp(p):
        return kb.at[pl.ds(pl.multiple_of(5 * FT + p * BLK, BLK), BLK)]

    def vp(p):
        return vb.at[pl.ds(pl.multiple_of(5 * FT + p * BLK, BLK), BLK), pl.ds(0, HD)]

    barrier = pltpu.get_barrier_semaphore()

    def hello(t, h):
        pl.semaphore_signal(barrier, inc=1, device_id=(t, h), device_id_type=MESH)

    vb[:, HD:] = jnp.ones((6 * FT, HD), jnp.bfloat16)

    hello(other, hd)
    for d in range(1, 8):
        hello(tm, lax.rem(hd + d, 8))
    for d in range(1, 4):
        hello(2 * (lax.rem(x + d, 4) * 4 + zh), hd)

    @pl.when(both(is0, has_prev))
    def _():
        hello(tm - 2, hd)
        hello(tm - 1, hd)

    @pl.when(both(is0, has_next))
    def _():
        hello(tm + 2, hd)

    @pl.when(both(is0, zh > 0))
    def _():
        hello(2 * x * 4, hd)

    own = (
        pltpu.make_async_copy(q_hbm, qb.at[pl.ds(0, 2 * FT)], lsem.at[0]),
        pltpu.make_async_copy(k_hbm, kb.at[pl.ds(0, 2 * FT)], lsem.at[1]),
        pltpu.make_async_copy(v_hbm, vb.at[pl.ds(0, 2 * FT), pl.ds(0, HD)], lsem.at[2]),
    )
    for cp in own:
        cp.start()
    root = both(is0, c == 0)
    sink_k = pltpu.make_async_copy(k_hbm.at[pl.ds(0, BLK)], kp(0), lsem.at[3])
    sink_v = pltpu.make_async_copy(v_hbm.at[pl.ds(0, BLK)], vp(0), lsem.at[4])

    @pl.when(root)
    def _():
        sink_k.start()
        sink_v.start()

    def bias(slot, frame):
        seen = jnp.logical_and(frame >= 1, jnp.logical_and(frame >= ws[slot], frame <= ge[slot]))
        return jnp.full((8, HD), jnp.where(seen, 0.0, HIDE), jnp.float32)

    base = 2 * tm
    part = 2 * other
    for s in range(2):
        bt[s * 6 + 0] = bias(s, base)
        bt[s * 6 + 1] = bias(s, base + 1)
        bt[s * 6 + 2] = bias(s, part)
        bt[s * 6 + 3] = bias(s, part + 1)
        bt[s * 6 + 4] = bias(s, 4 * c - 1)
        bt[s * 6 + 5] = jnp.zeros((8, HD), jnp.float32)
    for s in range(2):
        for m in range(2):
            bs[2 * s + m] = bias(s, 4 * c - 3 + m)

    mm[...] = jnp.full_like(mm, LOW)
    acc[...] = jnp.zeros_like(acc)
    more = 7 - first - last + 3 * (zh == 0).astype(jnp.int32) + 1
    pl.semaphore_wait(barrier, 8 + (1 - core) * more + core * (1 - last))

    par = [
        rc(k_hbm.at[pl.ds(0, FT)], kf(2), PK0, PK0, other, hd),
        rc(v_hbm.at[pl.ds(0, FT)], vf(2), PV0, PV0, other, hd),
        rc(k_hbm.at[pl.ds(FT, FT)], kf(3), PK1, PK1, other, hd),
        rc(v_hbm.at[pl.ds(FT, FT)], vf(3), PV1, PV1, other, hd),
    ]
    send_q = [
        rc(q_hbm.at[pl.ds(0, FT)], qb.at[pl.ds(2 * FT, FT)], RQ0, RQ0, tm - 2, hd),
        rc(bs, bt.at[pl.ds(12, 4)], RB, RB, tm - 2, hd),
        rc(q_hbm.at[pl.ds(FT, FT)], qb.at[pl.ds(3 * FT, FT)], RQ1, RQ1, tm - 2, hd),
    ]
    send_t = [
        rc(k_hbm.at[pl.ds(FT, FT)], kf(4), TK, TK, tm + 1, hd),
        rc(v_hbm.at[pl.ds(FT, FT)], vf(4), TV, TV, tm + 1, hd),
    ]

    @pl.when(both(is0, has_prev))
    def _():
        for cp in send_q:
            cp.start()

    @pl.when(both(is1, has_next))
    def _():
        for cp in send_t:
            cp.start()

    stage1 = []
    for d in range(1, 4):
        stage1.append(rc(k_hbm.at[pl.ds(d * BLK, BLK)], kp(d), S1S + 2 * d - 2, SK + d, 8 * d, hd))
        stage1.append(rc(v_hbm.at[pl.ds(d * BLK, BLK)], vp(d), S1S + 2 * d - 1, SV + d, 8 * d, hd))

    @pl.when(root)
    def _():
        for cp in stage1:
            cp.start()

    for cp in par[:2]:
        cp.start()

    @pl.when(is0)
    def _():
        for cp in par[2:]:
            cp.start()

    stage2 = []
    for d in range(1, 4):
        t = 2 * (x * 4 + d)
        stage2.append(rc(kp(x), kp(x), S2S + 2 * d - 2, SK + x, t, hd))
        stage2.append(rc(vp(x), vp(x), S2S + 2 * d - 1, SV + x, t, hd))
    stage3 = []
    n = S3S
    for d in range(4):
        for e in range(2):
            if d == 0 and e == 0:
                continue
            t = 2 * (lax.rem(x + d, 4) * 4 + zh) + e
            stage3.append(rc(kp(x), kp(x), n, SK + x, t, hd))
            stage3.append(rc(vp(x), vp(x), n + 1, SV + x, t, hd))
            n += 2

    for cp in own:
        cp.wait()

    @pl.when(root)
    def _():
        sink_k.wait()
        sink_v.wait()
        for cp in stage2:
            cp.start()

    def pick(i, a, b):
        r = a[0] + core * (b[0] - a[0])
        for m in range(1, len(a)):
            r = jnp.where(i == m, a[m] + core * (b[m] - a[m]), r)
        return r

    def item(i):
        qs = pick(i, Q0, Q1)
        ks = pick(i, K0, K1)
        qd = qs - 2 * last * lax.div(qs, 2)
        kd = ks - 4 * first * (lax.div(ks, 4) - lax.div(ks, 5))
        far = lax.div(qs, 2)
        bi = (1 - far) * (qs * 6 + ks) + far * (12 + (qs - 2) * 2 + ks - 1)
        return (pl.multiple_of(qs * FT, FT), pl.multiple_of(qd * FT, FT),
                pl.multiple_of(kd * FT, FT), bi)

    def scores(i, s_ref, x_ref):
        _, qd, kd, bi = item(i)
        s = lax.dot_general(qb[pl.ds(qd, FT), :], kb[pl.ds(kd, FT), :],
                            (((1,), (1,)), ((), ())), preferred_element_type=jnp.float32)
        s_ref[...] = s
        t = s[:, :HD]
        for l in range(HD, FT, HD):
            t = jnp.maximum(t, s[:, l:l + HD])
        top = jnp.broadcast_to(jnp.max(t, axis=1, keepdims=True), (FT, HD))
        x_ref[...] = top + bt[bi][0:1]

    def mix(i, s_ref, x_ref):
        qs, _, kd, bi = item(i)
        rows = pl.ds(qs, FT)
        old = mm[rows, :]
        new = jnp.maximum(old, x_ref[...])
        keep = jnp.exp2((old - new) * C)
        mm[rows, :] = new
        sub = new - bt[bi][0:1]
        w = [jnp.exp2((s_ref[:, l:l + HD] - sub) * C).astype(jnp.bfloat16)
             for l in range(0, FT, HD)]
        d = jnp.dot(jnp.concatenate(w, axis=1), vb[pl.ds(kd, FT), :],
                    preferred_element_type=jnp.float32)
        acc[rows, :HD] = acc[rows, :HD] * keep + d[:, :HD]
        acc[rows, HD:] = acc[rows, HD:] * keep + d[:, HD:]

    def run(start, count, mid):
        scores(start, s0, x0)

        def body(h, carry):
            i = start + 2 * h
            scores(i + 1, s1, x1)
            mix(i, s0, x0)
            mid(h)
            scores(jnp.minimum(i + 2, start + count - 1), s0, x0)
            mix(i + 1, s1, x1)
            return carry

        lax.fori_loop(0, count // 2, body, 0)

    def mid_a(h):
        @pl.when(both(is0, has_next, h == 1))
        def _():
            got(qb.at[pl.ds(2 * FT, FT)], RQ0)
            got(bt.at[pl.ds(12, 4)], RB)

        @pl.when(h == 1)
        def _():
            got(kf(2), PK0)
            got(vf(2), PV0)

        @pl.when(both(is0, zh == 0, x > 0, h == 1))
        def _():
            got(kp(x), SK + x)
            got(vp(x), SV + x)
            for cp in stage2:
                cp.start()

    run(0, 6, mid_a)

    eye = (lax.broadcasted_iota(jnp.int32, (HD, HD), 0)
           == lax.broadcasted_iota(jnp.int32, (HD, HD), 1))

    def give_back(s):
        def body(b, carry):
            r = pl.multiple_of((2 + s) * FT + b * HD, HD)
            o = pl.multiple_of(s * FT + b * HD, HD)
            den = acc[pl.ds(r, HD), HD:]
            ro[pl.ds(o, HD), :] = (acc[pl.ds(r, HD), :HD] / den).astype(jnp.bfloat16)
            lse = mm[pl.ds(r, HD), :] + jnp.log2(den) * (1.0 / C)
            rs[s * 6 + b] = jnp.broadcast_to(
                jnp.sum(jnp.where(eye, lse, 0.0), axis=0, keepdims=True), (8, HD))
            return carry

        lax.fori_loop(0, 6, body, 0)

    def returns(s):
        return (rc(ro.at[pl.ds(s * FT, FT)], reto.at[pl.ds(s * FT, FT)], RO + s, RO + s, tm + 2, hd),
                rc(rs.at[pl.ds(s * 6, 6)], rets.at[pl.ds(s * 6, 6)], RT + s, RT + s, tm + 2, hd))

    @pl.when(both(is0, has_next))
    def _():
        give_back(0)
        for cp in returns(0):
            cp.start()

    @pl.when(is0)
    def _():
        @pl.when(zh > 0)
        def _():
            got(kp(x), SK + x)
            got(vp(x), SV + x)

        for cp in stage3:
            cp.start()

    @pl.when(both(is0, has_next))
    def _():
        got(qb.at[pl.ds(3 * FT, FT)], RQ1)

    @pl.when(is1)
    def _():
        got(kf(3), PK1)
        got(vf(3), PV1)

    scores(6, s1, x1)
    mix(6, s1, x1)

    relay = (rc(kf(4), kf(4), TK, TK, other, hd), rc(vf(4), vf(4), TV, TV, other, hd))

    @pl.when(both(is0, has_next))
    def _():
        give_back(1)
        for cp in returns(1):
            cp.start()

    @pl.when(both(is0, has_prev))
    def _():
        got(kf(4), TK)
        got(vf(4), TV)
        for cp in relay:
            cp.start()

    def sink_in():
        for p in range(4):
            @pl.when(jnp.logical_or(is1, x != p))
            def _():
                got(kp(p), SK + p)
                got(vp(p), SV + p)

    @pl.when(is1)
    def _():
        sink_in()

    def mid_b(h):
        @pl.when(both(is0, h == 0))
        def _():
            sink_in()

        @pl.when(both(is1, has_prev, h == 0))
        def _():
            got(kf(4), TK)
            got(vf(4), TV)

    run(7, 4, mid_b)

    def finish(s):
        merged = both(is0, has_prev)

        @pl.when(merged)
        def _():
            got(reto.at[pl.ds(s * FT, FT)], RO + s)
            got(rets.at[pl.ds(s * 6, 6)], RT + s)

            def body(b, carry):
                r = pl.multiple_of(s * FT + b * HD, HD)
                row = jnp.broadcast_to(rets[s * 6 + b][0:1], (HD, HD))
                far = jnp.broadcast_to(
                    jnp.sum(jnp.where(eye, row, 0.0), axis=1, keepdims=True), (HD, HD))
                old = mm[pl.ds(r, HD), :]
                new = jnp.maximum(old, far)
                a = jnp.exp2((old - new) * C)
                b2 = jnp.exp2((far - new) * C)
                num = acc[pl.ds(r, HD), :HD] * a + reto[pl.ds(r, HD), :].astype(jnp.float32) * b2
                den = acc[pl.ds(r, HD), HD:] * a + b2
                att[pl.ds(r, HD), :] = (num / den).astype(jnp.bfloat16)
                return carry

            lax.fori_loop(0, 6, body, 0)

        @pl.when(jnp.logical_not(merged))
        def _():
            def body(b, carry):
                r = pl.multiple_of(s * FT + b * HD, HD)
                att[pl.ds(r, HD), :] = (acc[pl.ds(r, HD), :HD] / acc[pl.ds(r, HD), HD:]).astype(jnp.bfloat16)
                return carry

            lax.fori_loop(0, 6, body, 0)

    def block(j):
        return rc(att.at[pl.ds(j * BLK, BLK)], gath.at[hd], SH + j, RH + hd, tm, j)

    for s in range(2):
        finish(s)
        for j in range(4 * s, 4 * s + 4):
            @pl.when(j != hd)
            def _():
                block(j).start()

            @pl.when(j == hd)
            def _():
                gath[hd] = att[pl.ds(j * BLK, BLK), :]

    for e in range(8):
        @pl.when(e != hd)
        def _():
            got(gath.at[e], RH + e)
        out_ref[:, e * HD:(e + 1) * HD] = gath[e]

    for cp in par[:2]:
        cp.wait_send()

    @pl.when(is0)
    def _():
        for cp in par[2:]:
            cp.wait_send()
        for cp in stage3:
            cp.wait_send()

    @pl.when(both(is0, has_prev))
    def _():
        for cp in send_q:
            cp.wait_send()
        for cp in relay:
            cp.wait_send()

    @pl.when(both(is0, has_next))
    def _():
        for s in range(2):
            for cp in returns(s):
                cp.wait_send()

    @pl.when(both(is1, has_next))
    def _():
        for cp in send_t:
            cp.wait_send()

    @pl.when(root)
    def _():
        for cp in stage1:
            cp.wait_send()

    @pl.when(both(is0, zh == 0))
    def _():
        for cp in stage2:
            cp.wait_send()

    for j in range(8):
        @pl.when(j != hd)
        def _():
            block(j).wait_send()


def local(query_states, key_states, value_states, win_start, group_end, out_weight):
    rows = pl.pallas_call(
        kernel,
        out_shape=jax.ShapeDtypeStruct((BLK, 8 * HD), jnp.bfloat16),
        in_specs=[pl.BlockSpec(memory_space=pl.ANY)] * 3 + [pl.BlockSpec(memory_space=pltpu.SMEM)] * 2,
        out_specs=pl.BlockSpec(memory_space=pltpu.VMEM),
        scratch_shapes=[
            pltpu.VMEM((4 * FT, HD), jnp.bfloat16),
            pltpu.VMEM((6 * FT, HD), jnp.bfloat16),
            pltpu.VMEM((6 * FT, 2 * HD), jnp.bfloat16),
            pltpu.VMEM((4 * FT, 2 * HD), jnp.float32),
            pltpu.VMEM((4 * FT, HD), jnp.float32),
            pltpu.VMEM((FT, FT), jnp.float32),
            pltpu.VMEM((FT, FT), jnp.float32),
            pltpu.VMEM((FT, HD), jnp.float32),
            pltpu.VMEM((FT, HD), jnp.float32),
            pltpu.VMEM((16, 8, HD), jnp.float32),
            pltpu.VMEM((4, 8, HD), jnp.float32),
            pltpu.VMEM((2 * FT, HD), jnp.bfloat16),
            pltpu.VMEM((2 * FT, HD), jnp.bfloat16),
            pltpu.VMEM((12, 8, HD), jnp.float32),
            pltpu.VMEM((2 * FT, HD), jnp.bfloat16),
            pltpu.VMEM((12, 8, HD), jnp.float32),
            pltpu.VMEM((8, BLK, HD), jnp.bfloat16),
            pltpu.SemaphoreType.DMA((5,)),
            pltpu.SemaphoreType.DMA((47,)),
            pltpu.SemaphoreType.DMA((29,)),
        ],
        compiler_params=pltpu.CompilerParams(
            collective_id=0, has_side_effects=True, vmem_limit_bytes=60 * 1024 * 1024),
        name="attend",
    )(query_states, key_states, value_states, win_start, group_end)
    return jnp.dot(rows, out_weight, preferred_element_type=jnp.float32).astype(jnp.bfloat16)


def solution(mesh):
    in_specs = (P("tm", "head"), P("tm", "head"), P("tm", "head"), P("tm"), P("tm"), P())
    out_specs = P(("tm", "head"), None)
    return jax.shard_map(local, mesh=mesh, in_specs=in_specs, out_specs=out_specs, check_vma=False)
```

time: 345 us -> 45.4 us (0.13)
  the two profiles are of different devices: /device:TPU:8 before, /device:TPU:1 now
where the time goes in v1:
time: 45.4 us; the launch traced here: 45.2 us
  Pallas kernels  42.6 us (94%)
  matrix products  2.6 us (6%)
    pallas_call x1, Pallas kernels, local(): pl.pallas_call(kernel, out_shape=jax.ShapeDtypeStruct((BLK, 8 * HD), jnp....  42.6 us
    dot_general x1, matrix products, local(): jnp.dot(rows, out_weight, preferred_element_type=jnp.float32)  2.6 us

profile of v1, /device:TPU:1, one launch (start us, length us, event | category | flops | bytes accessed | tf_op | source)
XLA Modules:
  0.0 45.2 jit_solution(3622470295034461557)
XLA Ops:
  0.0 0.0 copy-start
  0.0 42.6 %attend.1 = bf16[192,1024]{1,0:T(8,128)(2,1)} custom-call(bf16[1536,128]{1,0:T(8,128)(2,1)} %q_hbm.1, bf16[1536,128]{1,0:T(8,128)(2,1)} %k_hbm.1, bf16[1536,128]{1,0:T(8,128)(2,1)} %v_hbm.1, s32[2]{0:T(128)} %ws.1, s32[2]{0:T(128)} %ge.1), custom_call_target="tpu_custom_call" | custom-call | tf_op jit(solution)/shard_map/attend/pallas_call | solution.py:465
  42.6 0.0 copy-done
  42.6 2.6 %convolution_convert_fusion = bf16[192,1536]{1,0:T(8,128)(2,1)} fusion(bf16[192,1024]{1,0:T(8,128)(2,1)} %attend.1, bf16[1024,1536]{1,0:T(8,128)(2,1)S(1)} %copy-done), kind=kOutput, calls=%fused_computation | convolution fusion | flops 604274688 | bytes 4128768 | tf_op jit(solution)/shard_map/dot_general | solution.py:496
Async XLA Ops:
  0.0 42.6 %copy-start = (bf16[1024,1536]{1,0:T(8,128)(2,1)S(1)}, bf16[1024,1536]{1,0:T(8,128)(2,1)}, u32[]{:S(2)}) copy-start(bf16[1024,1536]{1,0:T(8,128)(2,1)} %param.11) | copy-start | bytes 9437188

commit v2 on v1

--- a/solution.py
+++ b/solution.py
@@ -13,17 +13,17 @@
 LOW = -3.0e6
 MESH = pl.DeviceIdType.MESH
 
-Q0 = (0, 1, 0, 1, 2, 2, 3, 0, 1, 0, 1)
-K0 = (0, 0, 1, 1, 1, 2, 2, 4, 4, 5, 5)
-Q1 = (0, 1, 0, 1, 0, 1, 0, 1, 1, 0, 0)
-K1 = (0, 0, 1, 1, 2, 2, 3, 3, 5, 5, 4)
-
-PK0, PV0, PK1, PV1, TK, TV, RQ0, RQ1, RB, RO, RT, SK, SV, RH = (
-    0, 1, 2, 3, 4, 5, 6, 7, 8, 9, 11, 13, 17, 21)
-S1S, S2S, S3S, SH = 13, 19, 25, 39
-
-
-def kernel(q_hbm, k_hbm, v_hbm, ws, ge, out_ref, qb, kb, vb, acc, mm, s0, s1, x0, x1,
+Q0 = (0, 1, 0, 1, 2, 2, 0, 1, 3, 0, 1)
+K0 = (0, 0, 1, 1, 1, 2, 4, 4, 2, 5, 5)
+Q1 = (0, 1, 0, 1, 0, 1, 0, 1, 0, 0, 1)
+K1 = (0, 0, 1, 1, 2, 2, 3, 3, 4, 5, 5)
+
+PK0, PV0, PK1, PV1, TK, TV, RQ0, RQ1, RB, RO, RT, SP, SF, RH = (
+    0, 1, 2, 3, 4, 5, 6, 7, 8, 9, 11, 13, 17, 18)
+S1S, S2S, S3S, S4S, SH = 13, 20, 23, 26, 27
+
+
+def kernel(q_hbm, k_hbm, v_hbm, ws_hbm, ge_hbm, out_ref, ws, ge, qb, kb, vb, acc, mm, s0, x0,
            bt, bs, att, ro, rs, reto, rets, gath, lsem, ssem, rsem):
     tm = lax.axis_index("tm")
     hd = lax.axis_index("head")
@@ -73,27 +73,6 @@
     def hello(t, h):
         pl.semaphore_signal(barrier, inc=1, device_id=(t, h), device_id_type=MESH)
 
-    vb[:, HD:] = jnp.ones((6 * FT, HD), jnp.bfloat16)
-
-    hello(other, hd)
-    for d in range(1, 8):
-        hello(tm, lax.rem(hd + d, 8))
-    for d in range(1, 4):
-        hello(2 * (lax.rem(x + d, 4) * 4 + zh), hd)
-
-    @pl.when(both(is0, has_prev))
-    def _():
-        hello(tm - 2, hd)
-        hello(tm - 1, hd)
-
-    @pl.when(both(is0, has_next))
-    def _():
-        hello(tm + 2, hd)
-
-    @pl.when(both(is0, zh > 0))
-    def _():
-        hello(2 * x * 4, hd)
-
     own = (
         pltpu.make_async_copy(q_hbm, qb.at[pl.ds(0, 2 * FT)], lsem.at[0]),
         pltpu.make_async_copy(k_hbm, kb.at[pl.ds(0, 2 * FT)], lsem.at[1]),
@@ -101,19 +80,48 @@
     )
     for cp in own:
         cp.start()
+    limits = (pltpu.make_async_copy(ws_hbm, ws, lsem.at[4]), pltpu.make_async_copy(ge_hbm, ge, lsem.at[5]))
+    for cp in limits:
+        cp.start()
+
+    vb[:, HD:] = jnp.ones((6 * FT, HD), jnp.bfloat16)
+
+    hello(other, hd)
+    for d in range(1, 8):
+        hello(tm, lax.rem(hd + d, 8))
+    for d in range(1, 4):
+        hello(2 * (lax.rem(x + d, 4) * 4 + zh) + core, hd)
+
+    @pl.when(both(is0, has_prev))
+    def _():
+        hello(tm - 2, hd)
+        hello(tm - 1, hd)
+
+    @pl.when(both(is0, has_next))
+    def _():
+        hello(tm + 2, hd)
+
+    @pl.when(zh > 0)
+    def _():
+        hello(8 * x + core, hd)
+
+    @pl.when(both(is1, zh == 0, x > 0))
+    def _():
+        hello(0, hd)
+
     root = both(is0, c == 0)
     sink_k = pltpu.make_async_copy(k_hbm.at[pl.ds(0, BLK)], kp(0), lsem.at[3])
-    sink_v = pltpu.make_async_copy(v_hbm.at[pl.ds(0, BLK)], vp(0), lsem.at[4])
 
     @pl.when(root)
     def _():
         sink_k.start()
-        sink_v.start()
 
     def bias(slot, frame):
         seen = jnp.logical_and(frame >= 1, jnp.logical_and(frame >= ws[slot], frame <= ge[slot]))
         return jnp.full((8, HD), jnp.where(seen, 0.0, HIDE), jnp.float32)
 
+    for cp in limits:
+        cp.wait()
     base = 2 * tm
     part = 2 * other
     for s in range(2):
@@ -127,10 +135,9 @@
         for m in range(2):
             bs[2 * s + m] = bias(s, 4 * c - 3 + m)
 
-    mm[...] = jnp.full_like(mm, LOW)
-    acc[...] = jnp.zeros_like(acc)
-    more = 7 - first - last + 3 * (zh == 0).astype(jnp.int32) + 1
-    pl.semaphore_wait(barrier, 8 + (1 - core) * more + core * (1 - last))
+    low = (zh == 0).astype(jnp.int32)
+    head0 = first * (1 - core)
+    pl.semaphore_wait(barrier, 11 + 3 * low + 3 * head0 + (1 - core) * (2 - first - last) + core * (1 - last))
 
     par = [
         rc(k_hbm.at[pl.ds(0, FT)], kf(2), PK0, PK0, other, hd),
@@ -150,18 +157,18 @@
 
     @pl.when(both(is0, has_prev))
     def _():
-        for cp in send_q:
-            cp.start()
+        send_q[0].start()
+        send_q[1].start()
 
     @pl.when(both(is1, has_next))
     def _():
         for cp in send_t:
             cp.start()
 
-    stage1 = []
+    stage1 = [rc(v_hbm.at[pl.ds(0, BLK)], vp(0), S1S, SP, 1, hd)]
     for d in range(1, 4):
-        stage1.append(rc(k_hbm.at[pl.ds(d * BLK, BLK)], kp(d), S1S + 2 * d - 2, SK + d, 8 * d, hd))
-        stage1.append(rc(v_hbm.at[pl.ds(d * BLK, BLK)], vp(d), S1S + 2 * d - 1, SV + d, 8 * d, hd))
+        stage1.append(rc(k_hbm.at[pl.ds(d * BLK, BLK)], kp(d), S1S + 2 * d - 1, SP + d, 8 * d, hd))
+        stage1.append(rc(v_hbm.at[pl.ds(d * BLK, BLK)], vp(d), S1S + 2 * d, SP + d, 8 * d + 1, hd))
 
     @pl.when(root)
     def _():
@@ -176,21 +183,28 @@
         for cp in par[2:]:
             cp.start()
 
-    stage2 = []
-    for d in range(1, 4):
-        t = 2 * (x * 4 + d)
-        stage2.append(rc(kp(x), kp(x), S2S + 2 * d - 2, SK + x, t, hd))
-        stage2.append(rc(vp(x), vp(x), S2S + 2 * d - 1, SV + x, t, hd))
-    stage3 = []
-    n = S3S
-    for d in range(4):
-        for e in range(2):
-            if d == 0 and e == 0:
-                continue
-            t = 2 * (lax.rem(x + d, 4) * 4 + zh) + e
-            stage3.append(rc(kp(x), kp(x), n, SK + x, t, hd))
-            stage3.append(rc(vp(x), vp(x), n + 1, SV + x, t, hd))
-            n += 2
+    def by_core(f):
+        @pl.when(is0)
+        def _():
+            f(kp, kf)
+
+        @pl.when(is1)
+        def _():
+            f(vp, vf)
+
+    def stage2(piece):
+        return [rc(piece(x), piece(x), S2S + d - 1, SP + x, 2 * (x * 4 + d) + core, hd)
+                for d in range(1, 4)]
+
+    def stage3(piece):
+        return [rc(piece(x), piece(x), S3S + d - 1, SP + x,
+                   2 * (lax.rem(x + d, 4) * 4 + zh) + core, hd) for d in range(1, 4)]
+
+    def stage4(full):
+        return rc(full(5), full(5), S4S, SF, other, hd)
+
+    mm[...] = jnp.full_like(mm, LOW)
+    acc[...] = jnp.zeros_like(acc)
 
     for cp in own:
         cp.wait()
@@ -198,9 +212,6 @@
     @pl.when(root)
     def _():
         sink_k.wait()
-        sink_v.wait()
-        for cp in stage2:
-            cp.start()
 
     def pick(i, a, b):
         r = a[0] + core * (b[0] - a[0])
@@ -244,40 +255,6 @@
         acc[rows, :HD] = acc[rows, :HD] * keep + d[:, :HD]
         acc[rows, HD:] = acc[rows, HD:] * keep + d[:, HD:]
 
-    def run(start, count, mid):
-        scores(start, s0, x0)
-
-        def body(h, carry):
-            i = start + 2 * h
-            scores(i + 1, s1, x1)
-            mix(i, s0, x0)
-            mid(h)
-            scores(jnp.minimum(i + 2, start + count - 1), s0, x0)
-            mix(i + 1, s1, x1)
-            return carry
-
-        lax.fori_loop(0, count // 2, body, 0)
-
-    def mid_a(h):
-        @pl.when(both(is0, has_next, h == 1))
-        def _():
-            got(qb.at[pl.ds(2 * FT, FT)], RQ0)
-            got(bt.at[pl.ds(12, 4)], RB)
-
-        @pl.when(h == 1)
-        def _():
-            got(kf(2), PK0)
-            got(vf(2), PV0)
-
-        @pl.when(both(is0, zh == 0, x > 0, h == 1))
-        def _():
-            got(kp(x), SK + x)
-            got(vp(x), SV + x)
-            for cp in stage2:
-                cp.start()
-
-    run(0, 6, mid_a)
-
     eye = (lax.broadcasted_iota(jnp.int32, (HD, HD), 0)
            == lax.broadcasted_iota(jnp.int32, (HD, HD), 1))
 
@@ -298,71 +275,112 @@
         return (rc(ro.at[pl.ds(s * FT, FT)], reto.at[pl.ds(s * FT, FT)], RO + s, RO + s, tm + 2, hd),
                 rc(rs.at[pl.ds(s * 6, 6)], rets.at[pl.ds(s * 6, 6)], RT + s, RT + s, tm + 2, hd))
 
-    @pl.when(both(is0, has_next))
-    def _():
-        give_back(0)
-        for cp in returns(0):
-            cp.start()
-
-    @pl.when(is0)
-    def _():
-        @pl.when(zh > 0)
-        def _():
-            got(kp(x), SK + x)
-            got(vp(x), SV + x)
-
-        for cp in stage3:
-            cp.start()
-
-    @pl.when(both(is0, has_next))
-    def _():
-        got(qb.at[pl.ds(3 * FT, FT)], RQ1)
-
-    @pl.when(is1)
-    def _():
-        got(kf(3), PK1)
-        got(vf(3), PV1)
-
-    scores(6, s1, x1)
-    mix(6, s1, x1)
-
     relay = (rc(kf(4), kf(4), TK, TK, other, hd), rc(vf(4), vf(4), TV, TV, other, hd))
 
-    @pl.when(both(is0, has_next))
-    def _():
-        give_back(1)
-        for cp in returns(1):
-            cp.start()
-
-    @pl.when(both(is0, has_prev))
-    def _():
-        got(kf(4), TK)
-        got(vf(4), TV)
-        for cp in relay:
-            cp.start()
-
-    def sink_in():
-        for p in range(4):
-            @pl.when(jnp.logical_or(is1, x != p))
-            def _():
-                got(kp(p), SK + p)
-                got(vp(p), SV + p)
-
-    @pl.when(is1)
-    def _():
-        sink_in()
-
-    def mid_b(h):
-        @pl.when(both(is0, h == 0))
-        def _():
-            sink_in()
-
-        @pl.when(both(is1, has_prev, h == 0))
-        def _():
-            got(kf(4), TK)
-            got(vf(4), TV)
-
-    run(7, 4, mid_b)
+    def before(i):
+        @pl.when(i == 3)
+        def _():
+            @pl.when(zh == 0)
+            def _():
+                def f(piece, full):
+                    @pl.when(jnp.logical_not(root))
+                    def _():
+                        got(piece(x), SP + x)
+
+                    for cp in stage2(piece):
+                        cp.start()
+
+                by_core(f)
+
+        @pl.when(i == 4)
+        def _():
+            @pl.when(both(is0, has_prev))
+            def _():
+                send_q[0].wait_send()
+                send_q[2].start()
+
+            got(kf(2), PK0)
+            got(vf(2), PV0)
+
+            @pl.when(both(is0, has_next))
+            def _():
+                got(qb.at[pl.ds(2 * FT, FT)], RQ0)
+                got(bt.at[pl.ds(12, 4)], RB)
+
+        @pl.when(i == 6)
+        def _():
+            @pl.when(both(is0, has_next))
+            def _():
+                give_back(0)
+                for cp in returns(0):
+                    cp.start()
+
+            def f(piece, full):
+                @pl.when(zh > 0)
+                def _():
+                    got(piece(x), SP + x)
+
+                for cp in stage3(piece):
+                    cp.start()
+
+            by_core(f)
+
+            @pl.when(both(is0, has_prev))
+            def _():
+                got(kf(4), TK)
+                got(vf(4), TV)
+                for cp in relay:
+                    cp.start()
+
+            @pl.when(is1)
+            def _():
+                got(kf(3), PK1)
+                got(vf(3), PV1)
+
+        @pl.when(i == 8)
+        def _():
+            @pl.when(both(is0, has_next))
+            def _():
+                got(qb.at[pl.ds(3 * FT, FT)], RQ1)
+
+            @pl.when(both(is1, has_prev))
+            def _():
+                got(kf(4), TK)
+                got(vf(4), TV)
+
+        @pl.when(i == 9)
+        def _():
+            @pl.when(both(is0, has_next))
+            def _():
+                give_back(1)
+                for cp in returns(1):
+                    cp.start()
+
+            def f(piece, full):
+                for p in range(4):
+                    @pl.when(x != p)
+                    def _():
+                        got(piece(p), SP + p)
+
+                stage4(full).start()
+
+            by_core(f)
+
+            @pl.when(is0)
+            def _():
+                got(vf(5), SF)
+
+            @pl.when(is1)
+            def _():
+                got(kf(5), SF)
+
+    def step(i, carry):
+        before(i)
+        scores(i, s0, x0)
+        mix(i, s0, x0)
+        return carry
+
+    lax.fori_loop(0, 11, step, 0)
 
     def finish(s):
         merged = both(is0, has_prev)
@@ -424,12 +442,22 @@
     def _():
         for cp in par[2:]:
             cp.wait_send()
-        for cp in stage3:
+
+    def drain(piece, full):
+        for cp in stage3(piece):
             cp.wait_send()
+        stage4(full).wait_send()
+
+        @pl.when(zh == 0)
+        def _():
+            for cp in stage2(piece):
+                cp.wait_send()
+
+    by_core(drain)
 
     @pl.when(both(is0, has_prev))
     def _():
-        for cp in send_q:
+        for cp in send_q[1:]:
             cp.wait_send()
         for cp in relay:
             cp.wait_send()
@@ -448,11 +476,6 @@
     @pl.when(root)
     def _():
         for cp in stage1:
-            cp.wait_send()
-
-    @pl.when(both(is0, zh == 0))
-    def _():
-        for cp in stage2:
             cp.wait_send()
 
     for j in range(8):
@@ -465,17 +488,17 @@
     rows = pl.pallas_call(
         kernel,
         out_shape=jax.ShapeDtypeStruct((BLK, 8 * HD), jnp.bfloat16),
-        in_specs=[pl.BlockSpec(memory_space=pl.ANY)] * 3 + [pl.BlockSpec(memory_space=pltpu.SMEM)] * 2,
+        in_specs=[pl.BlockSpec(memory_space=pltpu.HBM)] * 5,
         out_specs=pl.BlockSpec(memory_space=pltpu.VMEM),
         scratch_shapes=[
+            pltpu.SMEM((2,), jnp.int32),
+            pltpu.SMEM((2,), jnp.int32),
             pltpu.VMEM((4 * FT, HD), jnp.bfloat16),
             pltpu.VMEM((6 * FT, HD), jnp.bfloat16),
             pltpu.VMEM((6 * FT, 2 * HD), jnp.bfloat16),
             pltpu.VMEM((4 * FT, 2 * HD), jnp.float32),
             pltpu.VMEM((4 * FT, HD), jnp.float32),
             pltpu.VMEM((FT, FT), jnp.float32),
-            pltpu.VMEM((FT, FT), jnp.float32),
-            pltpu.VMEM((FT, HD), jnp.float32),
             pltpu.VMEM((FT, HD), jnp.float32),
             pltpu.VMEM((16, 8, HD), jnp.float32),
             pltpu.VMEM((4, 8, HD), jnp.float32),
@@ -485,12 +508,12 @@
             pltpu.VMEM((2 * FT, HD), jnp.bfloat16),
             pltpu.VMEM((12, 8, HD), jnp.float32),
             pltpu.VMEM((8, BLK, HD), jnp.bfloat16),
-            pltpu.SemaphoreType.DMA((5,)),
-            pltpu.SemaphoreType.DMA((47,)),
-            pltpu.SemaphoreType.DMA((29,)),
+            pltpu.SemaphoreType.DMA((6,)),
+            pltpu.SemaphoreType.DMA((35,)),
+            pltpu.SemaphoreType.DMA((26,)),
         ],
         compiler_params=pltpu.CompilerParams(
-            collective_id=0, has_side_effects=True, vmem_limit_bytes=60 * 1024 * 1024),
+            collective_id=0, has_side_effects=True, vmem_limit_bytes=63000000),
         name="attend",
     )(query_states, key_states, value_states, win_start, group_end)
     return jnp.dot(rows, out_weight, preferred_element_type=jnp.float32).astype(jnp.bfloat16)

time: 45.4 us -> 43.8 us (0.965)
  the two profiles are of different devices: /device:TPU:1 before, /device:TPU:34 now
where the time goes in v2:
time: 43.8 us; the launch traced here: 43.7 us
  Pallas kernels  41.1 us (94%)
  matrix products  2.59 us (6%)
    pallas_call x1, Pallas kernels, local(): pl.pallas_call(kernel, out_shape=jax.ShapeDtypeStruct((BLK, 8 * HD), jnp....  41.1 us
    dot_general x1, matrix products, local(): jnp.dot(rows, out_weight, preferred_element_type=jnp.float32)  2.59 us

profile of v2, /device:TPU:34, one launch (start us, length us, event | category | flops | bytes accessed | tf_op | source)
XLA Modules:
  0.0 43.7 jit_solution(15686763693229818171)
XLA Ops:
  0.0 0.0 copy-start
  0.0 41.1 %attend.1 = bf16[192,1024]{1,0:T(8,128)(2,1)} custom-call(bf16[1536,128]{1,0:T(8,128)(2,1)} %q_hbm.1, bf16[1536,128]{1,0:T(8,128)(2,1)} %k_hbm.1, bf16[1536,128]{1,0:T(8,128)(2,1)} %v_hbm.1, s32[2]{0:T(128)} %ws_hbm.1, s32[2]{0:T(128)} %ge_hbm.1), custom_call_target="tpu_custom_call" | custom-call | tf_op jit(solution)/shard_map/attend/pallas_call | solution.py:488
  41.1 0.0 copy-done
  41.1 2.6 %convolution_convert_fusion = bf16[192,1536]{1,0:T(8,128)(2,1)} fusion(bf16[192,1024]{1,0:T(8,128)(2,1)} %attend.1, bf16[1024,1536]{1,0:T(8,128)(2,1)S(1)} %copy-done), kind=kOutput, calls=%fused_computation | convolution fusion | flops 604274688 | bytes 4128768 | tf_op jit(solution)/shard_map/dot_general | solution.py:519
Async XLA Ops:
  0.0 41.1 %copy-start = (bf16[1024,1536]{1,0:T(8,128)(2,1)S(1)}, bf16[1024,1536]{1,0:T(8,128)(2,1)}, u32[]{:S(2)}) copy-start(bf16[1024,1536]{1,0:T(8,128)(2,1)} %param.11) | copy-start | bytes 9437188

commit v3 on v2

--- a/solution.py
+++ b/solution.py
@@ -13,17 +13,17 @@
 LOW = -3.0e6
 MESH = pl.DeviceIdType.MESH
 
-Q0 = (0, 1, 0, 1, 2, 2, 0, 1, 3, 0, 1)
-K0 = (0, 0, 1, 1, 1, 2, 4, 4, 2, 5, 5)
-Q1 = (0, 1, 0, 1, 0, 1, 0, 1, 0, 0, 1)
-K1 = (0, 0, 1, 1, 2, 2, 3, 3, 4, 5, 5)
-
-PK0, PV0, PK1, PV1, TK, TV, RQ0, RQ1, RB, RO, RT, SP, SF, RH = (
-    0, 1, 2, 3, 4, 5, 6, 7, 8, 9, 11, 13, 17, 18)
-S1S, S2S, S3S, S4S, SH = 13, 20, 23, 26, 27
-
-
-def kernel(q_hbm, k_hbm, v_hbm, ws_hbm, ge_hbm, out_ref, ws, ge, qb, kb, vb, acc, mm, s0, x0,
+Q0 = (0, 1, 2, 2, 0, 3, 1, 0, 1, 0, 1)
+K0 = (0, 0, 1, 2, 1, 2, 1, 4, 4, 5, 5)
+Q1 = (0, 1, 0, 1, 0, 1, 0, 1, 1, 0, 0)
+K1 = (0, 0, 1, 1, 2, 2, 3, 3, 5, 5, 4)
+
+PK0, PV0, PK1, PV1, TK, TV, RQ0, RQ1, RB, RO, RT, SK, SV, RH = (
+    0, 1, 2, 3, 4, 5, 6, 7, 8, 9, 11, 13, 17, 21)
+S1S, S2S, S3S, S4S, SH = 13, 21, 27, 33, 41
+
+
+def kernel(q_hbm, k_hbm, v_hbm, ws_hbm, ge_hbm, out_ref, ws, ge, qb, kb, vb, acc, mm, s0, s1, x0, x1,
            bt, bs, att, ro, rs, reto, rets, gath, lsem, ssem, rsem):
     tm = lax.axis_index("tm")
     hd = lax.axis_index("head")
@@ -89,8 +89,10 @@
     hello(other, hd)
     for d in range(1, 8):
         hello(tm, lax.rem(hd + d, 8))
-    for d in range(1, 4):
-        hello(2 * (lax.rem(x + d, 4) * 4 + zh) + core, hd)
+    @pl.when(is1)
+    def _():
+        for d in range(1, 4):
+            hello(2 * (lax.rem(x + d, 4) * 4 + zh) + 1, hd)
 
     @pl.when(both(is0, has_prev))
     def _():
@@ -101,20 +103,19 @@
     def _():
         hello(tm + 2, hd)
 
-    @pl.when(zh > 0)
-    def _():
-        hello(8 * x + core, hd)
+    @pl.when(both(is1, lax.rem(zh, 2) == 1))
+    def _():
+        hello(8 * x + 1, hd)
+
+    @pl.when(both(is1, zh == 2))
+    def _():
+        hello(tm + 2, hd)
 
     @pl.when(both(is1, zh == 0, x > 0))
     def _():
         hello(0, hd)
 
     root = both(is0, c == 0)
-    sink_k = pltpu.make_async_copy(k_hbm.at[pl.ds(0, BLK)], kp(0), lsem.at[3])
-
-    @pl.when(root)
-    def _():
-        sink_k.start()
 
     def bias(slot, frame):
         seen = jnp.logical_and(frame >= 1, jnp.logical_and(frame >= ws[slot], frame <= ge[slot]))
@@ -136,8 +137,7 @@
             bs[2 * s + m] = bias(s, 4 * c - 3 + m)
 
     low = (zh == 0).astype(jnp.int32)
-    head0 = first * (1 - core)
-    pl.semaphore_wait(barrier, 11 + 3 * low + 3 * head0 + (1 - core) * (2 - first - last) + core * (1 - last))
+    pl.semaphore_wait(barrier, 8 + (1 - core) * (2 - last - first + 3 * first) + core * (3 + 2 * low + lax.div(zh, 3) + 1 - last))
 
     par = [
         rc(k_hbm.at[pl.ds(0, FT)], kf(2), PK0, PK0, other, hd),
@@ -162,56 +162,43 @@
 
     @pl.when(both(is1, has_next))
     def _():
-        for cp in send_t:
-            cp.start()
-
-    stage1 = [rc(v_hbm.at[pl.ds(0, BLK)], vp(0), S1S, SP, 1, hd)]
-    for d in range(1, 4):
-        stage1.append(rc(k_hbm.at[pl.ds(d * BLK, BLK)], kp(d), S1S + 2 * d - 1, SP + d, 8 * d, hd))
-        stage1.append(rc(v_hbm.at[pl.ds(d * BLK, BLK)], vp(d), S1S + 2 * d, SP + d, 8 * d + 1, hd))
+        send_t[0].start()
+
+    @pl.when(both(is1, has_next, zh > 0))
+    def _():
+        send_t[1].start()
+
+    stage1 = []
+    for d in range(4):
+        rows = pl.ds(d * BLK, BLK)
+        stage1.append(rc(k_hbm.at[rows], kp(d), S1S + 2 * d, SK + d, 8 * d + 1, hd))
+        stage1.append(rc(v_hbm.at[rows], vp(d), S1S + 2 * d + 1, SV + d, 8 * d + 1, hd))
 
     @pl.when(root)
     def _():
         for cp in stage1:
             cp.start()
 
-    for cp in par[:2]:
-        cp.start()
-
-    @pl.when(is0)
-    def _():
-        for cp in par[2:]:
-            cp.start()
-
-    def by_core(f):
-        @pl.when(is0)
-        def _():
-            f(kp, kf)
-
-        @pl.when(is1)
-        def _():
-            f(vp, vf)
-
-    def stage2(piece):
-        return [rc(piece(x), piece(x), S2S + d - 1, SP + x, 2 * (x * 4 + d) + core, hd)
-                for d in range(1, 4)]
-
-    def stage3(piece):
-        return [rc(piece(x), piece(x), S3S + d - 1, SP + x,
-                   2 * (lax.rem(x + d, 4) * 4 + zh) + core, hd) for d in range(1, 4)]
-
-    def stage4(full):
-        return rc(full(5), full(5), S4S, SF, other, hd)
+    stage2 = []
+    for d in (1, 3):
+        t = 2 * (x * 4 + d) + 1
+        stage2.append(rc(kp(x), kp(x), S2S + d - 1, SK + x, t, hd))
+        stage2.append(rc(vp(x), vp(x), S2S + d, SV + x, t, hd))
+    stage2b = (rc(kp(x), kp(x), S2S, SK + x, tm - 2, hd), rc(vp(x), vp(x), S2S + 1, SV + x, tm - 2, hd))
+    stage3 = []
+    for d in (2, 1, 3):
+        t = 2 * (lax.rem(x + d, 4) * 4 + zh) + 1
+        stage3.append(rc(kp(x), kp(x), S3S + 2 * d - 2, SK + x, t, hd))
+        stage3.append(rc(vp(x), vp(x), S3S + 2 * d - 1, SV + x, t, hd))
+
+    def stage4(p):
+        return (rc(kp(p), kp(p), S4S + 2 * p, SK + p, other, hd), rc(vp(p), vp(p), S4S + 2 * p + 1, SV + p, other, hd))
 
     mm[...] = jnp.full_like(mm, LOW)
     acc[...] = jnp.zeros_like(acc)
 
     for cp in own:
         cp.wait()
-
-    @pl.when(root)
-    def _():
-        sink_k.wait()
 
     def pick(i, a, b):
         r = a[0] + core * (b[0] - a[0])
@@ -277,111 +264,6 @@
 
     relay = (rc(kf(4), kf(4), TK, TK, other, hd), rc(vf(4), vf(4), TV, TV, other, hd))
 
-    def before(i):
-        @pl.when(i == 3)
-        def _():
-            @pl.when(zh == 0)
-            def _():
-                def f(piece, full):
-                    @pl.when(jnp.logical_not(root))
-                    def _():
-                        got(piece(x), SP + x)
-
-                    for cp in stage2(piece):
-                        cp.start()
-
-                by_core(f)
-
-        @pl.when(i == 4)
-        def _():
-            @pl.when(both(is0, has_prev))
-            def _():
-                send_q[0].wait_send()
-                send_q[2].start()
-
-            got(kf(2), PK0)
-            got(vf(2), PV0)
-
-            @pl.when(both(is0, has_next))
-            def _():
-                got(qb.at[pl.ds(2 * FT, FT)], RQ0)
-                got(bt.at[pl.ds(12, 4)], RB)
-
-        @pl.when(i == 6)
-        def _():
-            @pl.when(both(is0, has_next))
-            def _():
-                give_back(0)
-                for cp in returns(0):
-                    cp.start()
-
-            def f(piece, full):
-                @pl.when(zh > 0)
-                def _():
-                    got(piece(x), SP + x)
-
-                for cp in stage3(piece):
-                    cp.start()
-
-            by_core(f)
-
-            @pl.when(both(is0, has_prev))
-            def _():
-                got(kf(4), TK)
-                got(vf(4), TV)
-                for cp in relay:
-                    cp.start()
-
-            @pl.when(is1)
-            def _():
-                got(kf(3), PK1)
-                got(vf(3), PV1)
-
-        @pl.when(i == 8)
-        def _():
-            @pl.when(both(is0, has_next))
-            def _():
-                got(qb.at[pl.ds(3 * FT, FT)], RQ1)
-
-            @pl.when(both(is1, has_prev))
-            def _():
-                got(kf(4), TK)
-                got(vf(4), TV)
-
-        @pl.when(i == 9)
-        def _():
-            @pl.when(both(is0, has_next))
-            def _():
-                give_back(1)
-                for cp in returns(1):
-                    cp.start()
-
-            def f(piece, full):
-                for p in range(4):
-                    @pl.when(x != p)
-                    def _():
-                        got(piece(p), SP + p)
-
-                stage4(full).start()
-
-            by_core(f)
-
-            @pl.when(is0)
-            def _():
-                got(vf(5), SF)
-
-            @pl.when(is1)
-            def _():
-                got(kf(5), SF)
-
-    def step(i, carry):
-        before(i)
-        scores(i, s0, x0)
-        mix(i, s0, x0)
-        return carry
-
-    lax.fori_loop(0, 11, step, 0)
-
     def finish(s):
         merged = both(is0, has_prev)
 
@@ -418,7 +300,7 @@
     def block(j):
         return rc(att.at[pl.ds(j * BLK, BLK)], gath.at[hd], SH + j, RH + hd, tm, j)
 
-    for s in range(2):
+    def deliver(s):
         finish(s)
         for j in range(4 * s, 4 * s + 4):
             @pl.when(j != hd)
@@ -429,6 +311,131 @@
             def _():
                 gath[hd] = att[pl.ds(j * BLK, BLK), :]
 
+    def before(i):
+        @pl.when(i == 1 + 2 * core)
+        def _():
+            for cp in par[:2]:
+                cp.start()
+
+        @pl.when(both(is1, zh == 0, i == 3))
+        def _():
+            got(kp(x), SK + x)
+            got(vp(x), SV + x)
+            for cp in stage2[:2]:
+                cp.start()
+
+            @pl.when(has_next)
+            def _():
+                send_t[1].start()
+
+        @pl.when(both(is0, i == 2))
+        def _():
+            for cp in par[2:]:
+                cp.start()
+
+            @pl.when(has_prev)
+            def _():
+                send_q[0].wait_send()
+                send_q[2].start()
+
+            @pl.when(has_next)
+            def _():
+                got(qb.at[pl.ds(2 * FT, FT)], RQ0)
+                got(bt.at[pl.ds(12, 4)], RB)
+
+        @pl.when(i == 3 + core)
+        def _():
+            got(kf(2), PK0)
+            got(vf(2), PV0)
+
+        @pl.when(both(is0, has_next, i == 5))
+        def _():
+            give_back(0)
+            for cp in returns(0):
+                cp.start()
+            got(qb.at[pl.ds(3 * FT, FT)], RQ1)
+
+        @pl.when(both(is0, has_next, i == 7))
+        def _():
+            give_back(1)
+            for cp in returns(1):
+                cp.start()
+
+        @pl.when(both(is1, zh == 0, i == 5))
+        def _():
+            for cp in stage2[2:]:
+                cp.start()
+
+        @pl.when(both(is1, i == 6))
+        def _():
+            got(kf(3), PK1)
+            got(vf(3), PV1)
+
+        @pl.when(both(is0, has_prev, i == 7))
+        def _():
+            got(kf(4), TK)
+            got(vf(4), TV)
+            for cp in relay:
+                cp.start()
+
+        @pl.when(both(is1, i == 8))
+        def _():
+            @pl.when(zh > 0)
+            def _():
+                got(kp(x), SK + x)
+                got(vp(x), SV + x)
+
+            @pl.when(zh == 3)
+            def _():
+                for cp in stage2b:
+                    cp.start()
+
+            for cp in stage3:
+                cp.start()
+            for d in range(4):
+                p = lax.rem(x + d, 4)
+                if d:
+                    got(kp(p), SK + p)
+                    got(vp(p), SV + p)
+                for cp in stage4(p):
+                    cp.start()
+
+        @pl.when(both(is0, i == 9))
+        def _():
+            for p in range(4):
+                got(kp(p), SK + p)
+                got(vp(p), SV + p)
+
+        @pl.when(both(is1, i == 10))
+        def _():
+            deliver(1)
+
+            @pl.when(has_prev)
+            def _():
+                got(kf(4), TK)
+                got(vf(4), TV)
+
+    scores(0, s0, x0)
+
+    def step(h, carry):
+        i = 2 * h
+        before(i + 1)
+        scores(i + 1, s1, x1)
+        mix(i, s0, x0)
+        before(i + 2)
+        scores(i + 2, s0, x0)
+        mix(i + 1, s1, x1)
+        return carry
+
+    lax.fori_loop(0, 5, step, 0)
+    mix(10, s0, x0)
+
+    deliver(0)
+
+    @pl.when(is0)
+    def _():
+        deliver(1)
+
     for e in range(8):
         @pl.when(e != hd)
         def _():
@@ -443,17 +450,23 @@
         for cp in par[2:]:
             cp.wait_send()
 
-    def drain(piece, full):
-        for cp in stage3(piece):
-            cp.wait_send()
-        stage4(full).wait_send()
-
-        @pl.when(zh == 0)
-        def _():
-            for cp in stage2(piece):
+    @pl.when(is1)
+    def _():
+        for cp in stage3:
+            cp.wait_send()
+        for p in range(4):
+            for cp in stage4(p):
                 cp.wait_send()
 
-    by_core(drain)
+    @pl.when(both(is1, zh == 0))
+    def _():
+        for cp in stage2:
+            cp.wait_send()
+
+    @pl.when(both(is1, zh == 3))
+    def _():
+        for cp in stage2b:
+            cp.wait_send()
 
     @pl.when(both(is0, has_prev))
     def _():
@@ -485,6 +498,9 @@
 
 
 def local(query_states, key_states, value_states, win_start, group_end, out_weight):
+    query_states, key_states, value_states, win_start, group_end = (
+        pltpu.with_memory_space_constraint(a, pltpu.HBM)
+        for a in (query_states, key_states, value_states, win_start, group_end))
     rows = pl.pallas_call(
         kernel,
         out_shape=jax.ShapeDtypeStruct((BLK, 8 * HD), jnp.bfloat16),
@@ -499,6 +515,8 @@
             pltpu.VMEM((4 * FT, 2 * HD), jnp.float32),
             pltpu.VMEM((4 * FT, HD), jnp.float32),
             pltpu.VMEM((FT, FT), jnp.float32),
+            pltpu.VMEM((FT, FT), jnp.float32),
+            pltpu.VMEM((FT, HD), jnp.float32),
             pltpu.VMEM((FT, HD), jnp.float32),
             pltpu.VMEM((16, 8, HD), jnp.float32),
             pltpu.VMEM((4, 8, HD), jnp.float32),
@@ -509,11 +527,11 @@
             pltpu.VMEM((12, 8, HD), jnp.float32),
             pltpu.VMEM((8, BLK, HD), jnp.bfloat16),
             pltpu.SemaphoreType.DMA((6,)),
-            pltpu.SemaphoreType.DMA((35,)),
-            pltpu.SemaphoreType.DMA((26,)),
+            pltpu.SemaphoreType.DMA((49,)),
+            pltpu.SemaphoreType.DMA((29,)),
         ],
         compiler_params=pltpu.CompilerParams(
-            collective_id=0, has_side_effects=True, vmem_limit_bytes=63000000),
+            collective_id=0, has_side_effects=True, vmem_limit_bytes=36000000),
         name="attend",
     )(query_states, key_states, value_states, win_start, group_end)
     return jnp.dot(rows, out_weight, preferred_element_type=jnp.float32).astype(jnp.bfloat16)

time: 43.8 us -> 42.4 us (0.968)
  the two profiles are of different devices: /device:TPU:34 before, /device:TPU:62 now
where the time goes in v3:
time: 42.4 us
  Pallas kernels  40.7 us (96%)
  matrix products  1.6 us (4%)
    pallas_call x1, Pallas kernels, local(): pl.pallas_call(kernel, out_shape=jax.ShapeDtypeStruct((BLK, 8 * HD), jnp....  40.7 us
    dot_general x1, matrix products, local(): jnp.dot(rows, out_weight, preferred_element_type=jnp.float32)  1.6 us

profile of v3, /device:TPU:62, one launch (start us, length us, event | category | flops | bytes accessed | tf_op | source)
XLA Modules:
  0.0 42.4 jit_solution(4760721508945536604)
XLA Ops:
  0.0 0.0 copy-start
  0.0 40.7 %attend.1 = bf16[192,1024]{1,0:T(8,128)(2,1)S(1)} custom-call(bf16[1536,128]{1,0:T(8,128)(2,1)} %q_hbm.1, bf16[1536,128]{1,0:T(8,128)(2,1)} %k_hbm.1, bf16[1536,128]{1,0:T(8,128)(2,1)} %v_hbm.1, s32[2]{0:T(128)} %ws_hbm.1, s32[2]{0:T(128)} %ge_hbm.1), custom_call_target="tpu_custom_call" | custom-call | tf_op jit(solution)/shard_map/attend/pallas_call | solution.py:504
  40.7 0.0 copy-done
  40.8 1.6 %convolution_convert_fusion = bf16[192,1536]{1,0:T(8,128)(2,1)} fusion(bf16[192,1024]{1,0:T(8,128)(2,1)S(1)} %attend.1, bf16[1024,1536]{1,0:T(8,128)(2,1)S(1)} %copy-done), kind=kOutput, calls=%fused_computation | convolution fusion | flops 604274688 | bytes 4128768 | tf_op jit(solution)/shard_map/dot_general | solution.py:537
Async XLA Ops:
  0.0 40.7 %copy-start = (bf16[1024,1536]{1,0:T(8,128)(2,1)S(1)}, bf16[1024,1536]{1,0:T(8,128)(2,1)}, u32[]{:S(2)}) copy-start(bf16[1024,1536]{1,0:T(8,128)(2,1)} %param.11) | copy-start | bytes 9437188

commit v4 on v3

--- a/solution.py
+++ b/solution.py
@@ -103,13 +103,9 @@
     def _():
         hello(tm + 2, hd)
 
-    @pl.when(both(is1, lax.rem(zh, 2) == 1))
-    def _():
-        hello(8 * x + 1, hd)
-
-    @pl.when(both(is1, zh == 2))
-    def _():
-        hello(tm + 2, hd)
+    @pl.when(both(is1, zh > 0))
+    def _():
+        hello(tm - 2 - 4 * lax.div(zh, 3), hd)
 
     @pl.when(both(is1, zh == 0, x > 0))
     def _():
@@ -136,8 +132,8 @@
         for m in range(2):
             bs[2 * s + m] = bias(s, 4 * c - 3 + m)
 
-    low = (zh == 0).astype(jnp.int32)
-    pl.semaphore_wait(barrier, 8 + (1 - core) * (2 - last - first + 3 * first) + core * (3 + 2 * low + lax.div(zh, 3) + 1 - last))
+    low = 2 - zh + lax.div(zh, 3)
+    pl.semaphore_wait(barrier, 8 + (1 - core) * (2 - last - first + 3 * first) + core * (3 + low + 1 - last))
 
     par = [
         rc(k_hbm.at[pl.ds(0, FT)], kf(2), PK0, PK0, other, hd),
@@ -179,12 +175,8 @@
         for cp in stage1:
             cp.start()
 
-    stage2 = []
-    for d in (1, 3):
-        t = 2 * (x * 4 + d) + 1
-        stage2.append(rc(kp(x), kp(x), S2S + d - 1, SK + x, t, hd))
-        stage2.append(rc(vp(x), vp(x), S2S + d, SV + x, t, hd))
-    stage2b = (rc(kp(x), kp(x), S2S, SK + x, tm - 2, hd), rc(vp(x), vp(x), S2S + 1, SV + x, tm - 2, hd))
+    stage2 = (rc(kp(x), kp(x), S2S, SK + x, tm + 2, hd), rc(vp(x), vp(x), S2S + 1, SV + x, tm + 2, hd))
+    stage2b = (rc(kp(x), kp(x), S2S + 2, SK + x, tm + 6, hd), rc(vp(x), vp(x), S2S + 3, SV + x, tm + 6, hd))
     stage3 = []
     for d in (2, 1, 3):
         t = 2 * (lax.rem(x + d, 4) * 4 + zh) + 1
@@ -312,6 +304,10 @@
                 gath[hd] = att[pl.ds(j * BLK, BLK), :]
 
     def before(i):
+        @pl.when(both(is0, has_prev, i == 1))
+        def _():
+            send_q[2].start()
+
         @pl.when(i == 1 + 2 * core)
         def _():
             for cp in par[:2]:
@@ -321,7 +317,7 @@
         def _():
             got(kp(x), SK + x)
             got(vp(x), SV + x)
-            for cp in stage2[:2]:
+            for cp in stage2:
                 cp.start()
 
             @pl.when(has_next)
@@ -332,11 +328,6 @@
         def _():
             for cp in par[2:]:
                 cp.start()
-
-            @pl.when(has_prev)
-            def _():
-                send_q[0].wait_send()
-                send_q[2].start()
 
             @pl.when(has_next)
             def _():
@@ -359,11 +350,6 @@
         def _():
             give_back(1)
             for cp in returns(1):
-                cp.start()
-
-        @pl.when(both(is1, zh == 0, i == 5))
-        def _():
-            for cp in stage2[2:]:
                 cp.start()
 
         @pl.when(both(is1, i == 6))
@@ -385,13 +371,19 @@
                 got(kp(x), SK + x)
                 got(vp(x), SV + x)
 
-            @pl.when(zh == 3)
+            @pl.when(zh == 1)
+            def _():
+                for cp in stage2:
+                    cp.start()
+
+            for cp in stage3:
+                cp.start()
+
+            @pl.when(zh == 0)
             def _():
                 for cp in stage2b:
                     cp.start()
 
-            for cp in stage3:
-                cp.start()
             for d in range(4):
                 p = lax.rem(x + d, 4)
                 if d:
@@ -406,14 +398,10 @@
                 got(kp(p), SK + p)
                 got(vp(p), SV + p)
 
-        @pl.when(both(is1, i == 10))
-        def _():
-            deliver(1)
-
-            @pl.when(has_prev)
-            def _():
-                got(kf(4), TK)
-                got(vf(4), TV)
+        @pl.when(both(is1, has_prev, i == 10))
+        def _():
+            got(kf(4), TK)
+            got(vf(4), TV)
 
     scores(0, s0, x0)
 
@@ -431,10 +419,7 @@
     mix(10, s0, x0)
 
     deliver(0)
-
-    @pl.when(is0)
-    def _():
-        deliver(1)
+    deliver(1)
 
     for e in range(8):
         @pl.when(e != hd)
@@ -458,19 +443,19 @@
             for cp in stage4(p):
                 cp.wait_send()
 
+    @pl.when(both(is1, zh < 2))
+    def _():
+        for cp in stage2:
+            cp.wait_send()
+
     @pl.when(both(is1, zh == 0))
     def _():
-        for cp in stage2:
-            cp.wait_send()
-
-    @pl.when(both(is1, zh == 3))
-    def _():
         for cp in stage2b:
             cp.wait_send()
 
     @pl.when(both(is0, has_prev))
     def _():
-        for cp in send_q[1:]:
+        for cp in send_q:
             cp.wait_send()
         for cp in relay:
             cp.wait_send()

time: 42.4 us -> 40.7 us (0.960)
  the two profiles are of different devices: /device:TPU:62 before, /device:TPU:38 now
where the time goes in v4:
time: 40.7 us; the launch traced here: 40.6 us
  Pallas kernels  39 us (96%)
  matrix products  1.6 us (4%)
    pallas_call x1, Pallas kernels, local(): pl.pallas_call(kernel, out_shape=jax.ShapeDtypeStruct((BLK, 8 * HD), jnp....  39 us
    dot_general x1, matrix products, local(): jnp.dot(rows, out_weight, preferred_element_type=jnp.float32)  1.6 us

profile of v4, /device:TPU:38, one launch (start us, length us, event | category | flops | bytes accessed | tf_op | source)
XLA Modules:
  0.0 40.6 jit_solution(1765500983215253002)
XLA Ops:
  0.0 0.0 copy-start
  0.0 39.0 %attend.1 = bf16[192,1024]{1,0:T(8,128)(2,1)S(1)} custom-call(bf16[1536,128]{1,0:T(8,128)(2,1)} %q_hbm.1, bf16[1536,128]{1,0:T(8,128)(2,1)} %k_hbm.1, bf16[1536,128]{1,0:T(8,128)(2,1)} %v_hbm.1, s32[2]{0:T(128)} %ws_hbm.1, s32[2]{0:T(128)} %ge_hbm.1), custom_call_target="tpu_custom_call" | custom-call | tf_op jit(solution)/shard_map/attend/pallas_call | solution.py:489
  39.0 0.0 copy-done
  39.0 1.6 %convolution_convert_fusion = bf16[192,1536]{1,0:T(8,128)(2,1)} fusion(bf16[192,1024]{1,0:T(8,128)(2,1)S(1)} %attend.1, bf16[1024,1536]{1,0:T(8,128)(2,1)S(1)} %copy-done), kind=kOutput, calls=%fused_computation | convolution fusion | flops 604274688 | bytes 4128768 | tf_op jit(solution)/shard_map/dot_general | solution.py:522
Async XLA Ops:
  0.0 39.0 %copy-start = (bf16[1024,1536]{1,0:T(8,128)(2,1)S(1)}, bf16[1024,1536]{1,0:T(8,128)(2,1)}, u32[]{:S(2)}) copy-start(bf16[1024,1536]{1,0:T(8,128)(2,1)} %param.11) | copy-start | bytes 9437188

commit v5 on v4

--- a/solution.py
+++ b/solution.py
@@ -24,7 +24,7 @@
 
 
 def kernel(q_hbm, k_hbm, v_hbm, ws_hbm, ge_hbm, out_ref, ws, ge, qb, kb, vb, acc, mm, s0, s1, x0, x1,
-           bt, bs, att, ro, rs, reto, rets, gath, lsem, ssem, rsem):
+           bt, bs, att, ro, rs, reto, rets, gath, lsem, ssem, rsem, gate):
     tm = lax.axis_index("tm")
     hd = lax.axis_index("head")
     core = lax.rem(tm, 2)
@@ -103,9 +103,11 @@
     def _():
         hello(tm + 2, hd)
 
+    via = jnp.logical_and(x == 3, zh == 2)
+
     @pl.when(both(is1, zh > 0))
     def _():
-        hello(tm - 2 - 4 * lax.div(zh, 3), hd)
+        hello(8 * x + 1 + 6 * via.astype(jnp.int32), hd)
 
     @pl.when(both(is1, zh == 0, x > 0))
     def _():
@@ -132,7 +134,8 @@
         for m in range(2):
             bs[2 * s + m] = bias(s, 4 * c - 3 + m)
 
-    low = 2 - zh + lax.div(zh, 3)
+    edge = lax.div(x, 3)
+    low = (3 - edge) * (zh == 0).astype(jnp.int32) + edge * lax.div(zh, 3)
     pl.semaphore_wait(barrier, 8 + (1 - core) * (2 - last - first + 3 * first) + core * (3 + low + 1 - last))
 
     par = [
@@ -175,8 +178,12 @@
         for cp in stage1:
             cp.start()
 
-    stage2 = (rc(kp(x), kp(x), S2S, SK + x, tm + 2, hd), rc(vp(x), vp(x), S2S + 1, SV + x, tm + 2, hd))
-    stage2b = (rc(kp(x), kp(x), S2S + 2, SK + x, tm + 6, hd), rc(vp(x), vp(x), S2S + 3, SV + x, tm + 6, hd))
+    stage2 = []
+    for d in (2, 1):
+        stage2.append(rc(kp(x), kp(x), S2S + 2 * d, SK + x, tm + 2 * d, hd))
+        stage2.append(rc(vp(x), vp(x), S2S + 2 * d + 1, SV + x, tm + 2 * d, hd))
+    stage2b = (rc(kp(x), kp(x), S2S, SK + x, tm + 6, hd), rc(vp(x), vp(x), S2S + 1, SV + x, tm + 6, hd))
+    stage2c = (rc(kp(x), kp(x), S2S, SK + x, tm - 2, hd), rc(vp(x), vp(x), S2S + 1, SV + x, tm - 2, hd))
     stage3 = []
     for d in (2, 1, 3):
         t = 2 * (lax.rem(x + d, 4) * 4 + zh) + 1
@@ -290,18 +297,20 @@
             lax.fori_loop(0, 6, body, 0)
 
     def block(j):
-        return rc(att.at[pl.ds(j * BLK, BLK)], gath.at[hd], SH + j, RH + hd, tm, j)
+        return rc(att.at[pl.ds(pl.multiple_of(j * BLK, BLK), BLK)], gath.at[hd], SH + j, RH + hd, tm, j)
 
     def deliver(s):
         finish(s)
-        for j in range(4 * s, 4 * s + 4):
+        for d in (2, 1, 3, 0):
+            j = 4 * s + lax.rem(hd + d, 4)
+
             @pl.when(j != hd)
             def _():
                 block(j).start()
 
             @pl.when(j == hd)
             def _():
-                gath[hd] = att[pl.ds(j * BLK, BLK), :]
+                gath[hd] = att[pl.ds(pl.multiple_of(j * BLK, BLK), BLK), :]
 
     def before(i):
         @pl.when(both(is0, has_prev, i == 1))
@@ -317,7 +326,7 @@
         def _():
             got(kp(x), SK + x)
             got(vp(x), SV + x)
-            for cp in stage2:
+            for cp in stage2[2:]:
                 cp.start()
 
             @pl.when(has_next)
@@ -350,6 +359,11 @@
         def _():
             give_back(1)
             for cp in returns(1):
+                cp.start()
+
+        @pl.when(both(is1, zh == 0, x < 3, i == 7))
+        def _():
+            for cp in stage2[:2]:
                 cp.start()
 
         @pl.when(both(is1, i == 6))
@@ -371,9 +385,9 @@
                 got(kp(x), SK + x)
                 got(vp(x), SV + x)
 
-            @pl.when(zh == 1)
-            def _():
-                for cp in stage2:
+            @pl.when(both(zh == 3, x == 3))
+            def _():
+                for cp in stage2c:
                     cp.start()
 
             for cp in stage3:
@@ -419,6 +433,17 @@
     mix(10, s0, x0)
 
     deliver(0)
+
+    @pl.when(both(is0, has_next, hd < 4))
+    def _():
+        for cp in returns(1):
+            cp.wait_send()
+        pl.semaphore_signal(gate, inc=1, device_id=(other, hd), device_id_type=MESH)
+
+    @pl.when(both(is1, has_next, hd < 4))
+    def _():
+        pl.semaphore_wait(gate, 1)
+
     deliver(1)
 
     for e in range(8):
@@ -443,16 +468,23 @@
             for cp in stage4(p):
                 cp.wait_send()
 
-    @pl.when(both(is1, zh < 2))
-    def _():
-        for cp in stage2:
-            cp.wait_send()
-
     @pl.when(both(is1, zh == 0))
     def _():
+        for cp in stage2[2:]:
+            cp.wait_send()
         for cp in stage2b:
             cp.wait_send()
 
+    @pl.when(both(is1, zh == 0, x < 3))
+    def _():
+        for cp in stage2[:2]:
+            cp.wait_send()
+
+    @pl.when(both(is1, zh == 3, x == 3))
+    def _():
+        for cp in stage2c:
+            cp.wait_send()
+
     @pl.when(both(is0, has_prev))
     def _():
         for cp in send_q:
@@ -462,9 +494,13 @@
 
     @pl.when(both(is0, has_next))
     def _():
-        for s in range(2):
-            for cp in returns(s):
-                cp.wait_send()
+        for cp in returns(0):
+            cp.wait_send()
+
+    @pl.when(both(is0, has_next, hd >= 4))
+    def _():
+        for cp in returns(1):
+            cp.wait_send()
 
     @pl.when(both(is1, has_next))
     def _():
@@ -514,6 +550,7 @@
             pltpu.SemaphoreType.DMA((6,)),
             pltpu.SemaphoreType.DMA((49,)),
             pltpu.SemaphoreType.DMA((29,)),
+            pltpu.SemaphoreType.REGULAR,
         ],
         compiler_params=pltpu.CompilerParams(
             collective_id=0, has_side_effects=True, vmem_limit_bytes=36000000),

time: 40.7 us -> 40.9 us (level)
  no operation moved by 1% of the time
where the time goes in v5:
time: 40.9 us; the launch traced here: 40.8 us
  Pallas kernels  39.2 us (96%)
  matrix products  1.6 us (4%)
    pallas_call x1, Pallas kernels, local(): pl.pallas_call(kernel, out_shape=jax.ShapeDtypeStruct((BLK, 8 * HD), jnp....  39.2 us
    dot_general x1, matrix products, local(): jnp.dot(rows, out_weight, preferred_element_type=jnp.float32)  1.6 us

profile of v5, /device:TPU:38, one launch (start us, length us, event | category | flops | bytes accessed | tf_op | source)
XLA Modules:
  0.0 40.8 jit_solution(4708048540766071899)
XLA Ops:
  0.0 0.0 copy-start
  0.0 39.2 %attend.1 = bf16[192,1024]{1,0:T(8,128)(2,1)S(1)} custom-call(bf16[1536,128]{1,0:T(8,128)(2,1)} %q_hbm.1, bf16[1536,128]{1,0:T(8,128)(2,1)} %k_hbm.1, bf16[1536,128]{1,0:T(8,128)(2,1)} %v_hbm.1, s32[2]{0:T(128)} %ws_hbm.1, s32[2]{0:T(128)} %ge_hbm.1), custom_call_target="tpu_custom_call" | custom-call | tf_op jit(solution)/shard_map/attend/pallas_call | solution.py:525
  39.2 0.0 copy-done
  39.2 1.6 %convolution_convert_fusion = bf16[192,1536]{1,0:T(8,128)(2,1)} fusion(bf16[192,1024]{1,0:T(8,128)(2,1)S(1)} %attend.1, bf16[1024,1536]{1,0:T(8,128)(2,1)S(1)} %copy-done), kind=kOutput, calls=%fused_computation | convolution fusion | flops 604274688 | bytes 4128768 | tf_op jit(solution)/shard_map/dot_general | solution.py:559
Async XLA Ops:
  0.0 39.2 %copy-start = (bf16[1024,1536]{1,0:T(8,128)(2,1)S(1)}, bf16[1024,1536]{1,0:T(8,128)(2,1)}, u32[]{:S(2)}) copy-start(bf16[1024,1536]{1,0:T(8,128)(2,1)} %param.11) | copy-start | bytes 9437188

commit v6 on v4

--- a/solution.py
+++ b/solution.py
@@ -290,18 +290,20 @@
             lax.fori_loop(0, 6, body, 0)
 
     def block(j):
-        return rc(att.at[pl.ds(j * BLK, BLK)], gath.at[hd], SH + j, RH + hd, tm, j)
+        return rc(att.at[pl.ds(pl.multiple_of(j * BLK, BLK), BLK)], gath.at[hd], SH + j, RH + hd, tm, j)
 
     def deliver(s):
         finish(s)
-        for j in range(4 * s, 4 * s + 4):
+        for d in (2, 1, 3, 0):
+            j = 4 * s + lax.rem(hd + d, 4)
+
             @pl.when(j != hd)
             def _():
                 block(j).start()
 
             @pl.when(j == hd)
             def _():
-                gath[hd] = att[pl.ds(j * BLK, BLK), :]
+                gath[hd] = att[pl.ds(pl.multiple_of(j * BLK, BLK), BLK), :]
 
     def before(i):
         @pl.when(both(is0, has_prev, i == 1))

time: 40.7 us -> 40.6 us (level)
  no operation moved by 1% of the time
where the time goes in v6:
time: 40.6 us; the launch traced here: 40.5 us
  Pallas kernels  38.9 us (96%)
  matrix products  1.6 us (4%)
    pallas_call x1, Pallas kernels, local(): pl.pallas_call(kernel, out_shape=jax.ShapeDtypeStruct((BLK, 8 * HD), jnp....  38.9 us
    dot_general x1, matrix products, local(): jnp.dot(rows, out_weight, preferred_element_type=jnp.float32)  1.6 us

profile of v6, /device:TPU:38, one launch (start us, length us, event | category | flops | bytes accessed | tf_op | source)
XLA Modules:
  0.0 40.5 jit_solution(7289214264556577126)
XLA Ops:
  0.0 0.0 copy-start
  0.0 38.9 %attend.1 = bf16[192,1024]{1,0:T(8,128)(2,1)S(1)} custom-call(bf16[1536,128]{1,0:T(8,128)(2,1)} %q_hbm.1, bf16[1536,128]{1,0:T(8,128)(2,1)} %k_hbm.1, bf16[1536,128]{1,0:T(8,128)(2,1)} %v_hbm.1, s32[2]{0:T(128)} %ws_hbm.1, s32[2]{0:T(128)} %ge_hbm.1), custom_call_target="tpu_custom_call" | custom-call | tf_op jit(solution)/shard_map/attend/pallas_call | solution.py:491
  38.9 0.0 copy-done
  38.9 1.6 %convolution_convert_fusion = bf16[192,1536]{1,0:T(8,128)(2,1)} fusion(bf16[192,1024]{1,0:T(8,128)(2,1)S(1)} %attend.1, bf16[1024,1536]{1,0:T(8,128)(2,1)S(1)} %copy-done), kind=kOutput, calls=%fused_computation | convolution fusion | flops 604274688 | bytes 4128768 | tf_op jit(solution)/shard_map/dot_general | solution.py:524
Async XLA Ops:
  0.0 38.9 %copy-start = (bf16[1024,1536]{1,0:T(8,128)(2,1)S(1)}, bf16[1024,1536]{1,0:T(8,128)(2,1)}, u32[]{:S(2)}) copy-start(bf16[1024,1536]{1,0:T(8,128)(2,1)} %param.11) | copy-start | bytes 9437188
